TPU v7x, 512 devices: a whole 4x4x16 slice. The times are simulated.
512 devices in a mesh: node: 64 (over y, z), local: 8 (over x, core).
Axes of the slice: x: 4, y: 4, z: 16, core: 2. Of those that a mesh axis runs over, the one named last changes fastest.
Arguments:
- grad_out: bfloat16 [65536, 3584], P(('node', 'local')), may hold values from -6 to 6
- expert_ids: int32 [65536, 8], P(('node', 'local')), may hold values from 0 to 255, as said below
- gate_weights: float32 [65536, 8], P(('node', 'local')), may hold values from 0.05 to 0.35
- saved_hidden: bfloat16 [64, 1024, 1024], P('node', None, 'local'), may hold values from -0.59765625 to 0.59765625
- down_weight: bfloat16 [64, 1024, 3584], P('node', 'local'), may hold values from -0.1875 to 0.1875
- second_moment: bfloat16 [64, 1024, 3584], P('node', 'local'), may hold values from 0.0019989014 to 0.25
Outputs:
- gate_weight_gradient: float32 [65536, 8], P(('node', 'local'))
- hidden_grad: bfloat16 [64, 1024, 1024], P('node', None, 'local')
- new_weight: bfloat16 [64, 1024, 3584], P('node', 'local')
- new_second: bfloat16 [64, 1024, 3584], P('node', 'local')
Inputs may be any that keep to these rules, and one draw needn't show every extreme that they name: `expert_ids`: each row names 8 different experts on at most 4 nodes (node = id // 4), two on each; at most one per row is in flight (id % 4 == 0). Among the rows of one device at most 2 name the in-flight expert of any one node, and in every draw some node receives exactly 2 from every device.
All inputs are finite; a program needn't handle non-finite values.
Results may differ from a plain program's by a relative error of at most 0.0051.
Values may be sent and summed in bfloat16 or wider, within the bound.
No kernel may reach another device: no remote copies, remote signals or barrier semaphores. Data moves between devices by JAX's collectives and lax.ppermute only.
A program may use at most 128 MiB of HBM per device.

v0:
```python
import jax
import jax.numpy as jnp
from jax import lax
from jax.sharding import PartitionSpec as P

EXPERTS_PER_HOST = 4
CAP = 2
beta_second = 0.95
learn_rate = 0.002
decay_rate = 0.1
epsilon = 1e-08
correct_second = 0.994079470779666


def route(picked_experts, gate_values, node_count):
    transit_rows = picked_experts % EXPERTS_PER_HOST == 0
    row_present = jnp.any(transit_rows, 1)
    destination_node = jnp.sum(jnp.where(transit_rows, picked_experts // EXPERTS_PER_HOST, 0), 1)
    tokens = picked_experts.shape[0]
    same = (
        (destination_node[:, None] == destination_node[None, :])
        & row_present[None, :]
        & (jnp.arange(tokens)[None, :] < jnp.arange(tokens)[:, None])
    )
    within_rank = jnp.sum(same.astype(jnp.int32), 1)
    slot_index = destination_node * CAP + within_rank
    expert_location = (
        jnp.arange(node_count * CAP, dtype=jnp.int32)[:, None] == slot_index[None, :]
    ) & row_present[None, :]
    matched_gate = jnp.sum(jnp.where(transit_rows, gate_values, 0.0), 1).astype(jnp.bfloat16)
    return (expert_location, transit_rows, row_present, matched_gate.astype(jnp.float32))


def on_device(grad_out, expert_ids, gate_weights, saved_hidden, down_weight, second_moment):
    node_count = lax.axis_size("node")
    members = lax.axis_size("local")
    feature_count = grad_out.shape[1]
    expert_location, transit_rows, row_present, gate = route(expert_ids, gate_weights, node_count)
    slot_gate = jnp.sum(jnp.where(expert_location, gate[None, :], 0.0), 1)
    picked = jnp.dot(
        expert_location.astype(jnp.bfloat16), grad_out, preferred_element_type=jnp.float32
    )
    scaled_out = (slot_gate[:, None] * picked).astype(jnp.bfloat16)
    arrived = lax.all_to_all(
        scaled_out.reshape(node_count, CAP, feature_count),
        "node",
        split_axis=0,
        concat_axis=0,
        tiled=True,
    )
    scaled = lax.all_gather(
        arrived.reshape(node_count * CAP, feature_count), "local", axis=0, tiled=True
    )
    weight_now = down_weight[0]
    hidden_now = saved_hidden[0]
    hidden_f = lax.dot_general(
        scaled, weight_now, (((1,), (1,)), ((), ())), preferred_element_type=jnp.float32
    )
    slot_score = jnp.sum(hidden_f * hidden_now.astype(jnp.float32), 1)
    grad = lax.dot_general(
        hidden_now, scaled, (((0,), (0,)), ((), ())), preferred_element_type=jnp.float32
    )
    second_new = (
        beta_second * second_moment[0].astype(jnp.float32) + (1.0 - beta_second) * grad * grad
    )
    weight_f = weight_now.astype(jnp.float32)
    update = grad / (jnp.sqrt(second_new / correct_second) + epsilon) + decay_rate * weight_f
    weight_new = weight_f - learn_rate * update
    score_terms = slot_score.reshape(members, node_count * CAP)
    summed = lax.psum(score_terms, "local")
    own_terms = lax.dynamic_slice_in_dim(summed, lax.axis_index("local"), 1, 0)
    returned = lax.all_to_all(
        own_terms.reshape(node_count, CAP), "node", split_axis=0, concat_axis=0, tiled=True
    )
    returned_flat = returned.reshape(node_count * CAP)
    token_score = jnp.sum(jnp.where(expert_location, returned_flat[:, None], 0.0), 0)
    token_gradient = jnp.where(row_present, token_score / jnp.where(row_present, gate, 1.0), 0.0)
    gate_weight_gradient = jnp.where(transit_rows, token_gradient[:, None], 0.0)
    return (
        gate_weight_gradient,
        hidden_f.astype(jnp.bfloat16)[None],
        weight_new.astype(jnp.bfloat16)[None],
        second_new.astype(jnp.bfloat16)[None],
    )


def solution(mesh):
    return jax.shard_map(
        on_device,
        mesh=mesh,
        in_specs=(
            P(("node", "local"), None),
            P(("node", "local"), None),
            P(("node", "local"), None),
            P("node", None, "local"),
            P("node", "local", None),
            P("node", "local", None),
        ),
        out_specs=(
            P(("node", "local"), None),
            P("node", None, "local"),
            P("node", "local", None),
            P("node", "local", None),
        ),
        check_vma=False,
    )
```

profile of v0, /device:TPU:8, one launch (start us, length us, event | category | flops | bytes accessed | tf_op | source)
XLA Modules:
  0.0 181.2 jit_solution(6624401985966689629)
XLA Ops:
  7.2 0.0 copy-start
  7.2 0.0 all-gather.2.cloned.1.call-start
  7.2 0.8 fusion.18
  8.0 0.7 select_reduce_fusion.2
  8.7 0.0 copy-start.5
  8.7 0.2 convert_reduce_fusion
  8.9 0.1 select_reduce_fusion.1
  9.0 0.3 copy-done.5
  9.3 0.0 copy-done
  9.3 0.4 fusion
  9.7 0.3 reshape.51
  10.1 66.9 %all_to_all.14 = bf16[64,2,3584]{2,1,0:T(2,128)(2,1)S(1)} all-to-all(bf16[64,2,3584]{2,1,0:T(2,128)(2,1)S(1)} %reshape.51), channel_id=1, replica_groups=mesh['node'=64,'local'=8] {'node'}, dimensions={0} | all-to-all | bytes 1835008 | tf_op jit(solution)/shard_map/all_to_all | solution.py:44
  77.0 0.0 copy-start.4
  77.0 0.0 copy-start.1
  77.0 1.3 reshape.52
  78.3 0.0 copy-start.2
  78.3 0.0 all-gather.2.cloned.1.call-update
  78.3 0.0 copy-done.4
  78.3 0.1 copy.30
  78.5 0.0 copy-done.1
  78.5 1.3 copy.32
  79.7 0.0 copy-done.2
  79.7 1.3 copy.29
  81.0 0.0 copy-start.3
  81.0 42.7 %all-gather.2.cloned.1.call-done = bf16[1024,3584]{1,0:T(8,128)(2,1)} async-done(((bf16[128,3584]{1,0:T(8,128)(2,1)}), bf16[1024,3584]{1,0:T(8,128)(2,1)}) %all-gather.2.cloned.1.call-update) | async-done | bytes 7340048 | tf_op jit(solution)/shard_map/all_gather | solution.py:51
  123.7 5.5 %convert_bitcast_fusion = (bf16[1,1024,128]{1,2,0:T(8,128)(2,1)S(1)}, f32[1024]{0:T(1024)S(1)}) fusion(bf16[1,1024,128]{1,2,0:T(8,128)(2,1)S(1)} %copy.30, bf16[1024,3584]{1,0:T(8,128)(2,1)} %all-gather.2.cloned.1.call-done, bf16[1,128,3584]{2,1,0:T(8,128)(2,1)S(1)} %copy-done.2), kind=kOutput, calls=%fused_computation.17 | convolution fusion | flops 940047360 | bytes 8785920 | tf_op jit(solution)/shard_map/dot_general | solution.py:56
  129.2 13.2 %psum.7 = f32[8,128]{1,0:T(8,128)S(1)} all-reduce(f32[8,128]{1,0:T(8,128)S(1)} %bitcast.41), channel_id=1, replica_groups=mesh['node'=64,'local'=8] {'local'}, use_global_device_ids=true, to_apply=%region_6.7 | all-reduce | flops 1024 | bytes 8192 | tf_op jit(solution)/shard_map/psum | solution.py:70
  142.4 0.7 all_to_all.10
  143.2 15.8 %all-to-all-start.1 = ((f32[64,1,2]{2,1,0:T(1,128)}), f32[64,1,2]{2,1,0:T(1,128)S(1)}, u32[]{:S(2)}, u32[]{:S(2)}) async-start(f32[64,1,2]{2,1,0:T(1,128)} %bitcast.3), calls=%async_computation.1 | async-start | bytes 65536 | tf_op jit(solution)/shard_map/all_to_all | solution.py:72
  158.9 0.0 copy-done.3
  158.9 7.2 %fusion.6 = (bf16[1,128,3584]{1,2,0:T(8,128)(2,1)}, bf16[1,128,3584]{1,2,0:T(8,128)(2,1)S(1)}) fusion(bf16[1,128,3584]{1,2,0:T(8,128)(2,1)S(1)} %copy-done.3, bf16[1,128,3584]{1,2,0:T(8,128)(2,1)} %copy.29, bf16[1024,3584]{1,0:T(8,128)(2,1)} %all-gather.2.cloned.1.call-done, bf16[1,1024,128]{2,1,0:T(8,128)(2,1)S(1)} %copy-done.4), kind=kOutput, calls=%fused_computation.11 | convolution fusion | flops 946405376 | bytes 11272192 | tf_op jit(solution)/shard_map/dot_general | solution.py:60
  166.1 0.8 copy.33
  167.0 0.0 copy-start.6
  167.0 2.2 %copy.35 = bf16[1,128,3584]{2,1,0:T(8,128)(2,1)} copy(bf16[1,128,3584]{1,2,0:T(8,128)(2,1)} %get-tuple-element.22) | data formatting | bytes 1835008
  169.2 1.3 copy.34
  170.5 1.8 %all-to-all-done.1 = f32[64,1,2]{2,1,0:T(1,128)S(1)} async-done(((f32[64,1,2]{2,1,0:T(1,128)}), f32[64,1,2]{2,1,0:T(1,128)S(1)}, u32[]{:S(2)}, u32[]{:S(2)}) %all-to-all-start.1) | async-done | bytes 544 | tf_op jit(solution)/shard_map/all_to_all | solution.py:72
  172.3 0.5 broadcast.39
  172.8 0.7 reduce.7
  173.5 0.1 broadcast_in_dim.70
  173.7 0.1 select_reduce_fusion
  173.8 0.0 copy-done.6
  173.8 0.6 broadcast_select_fusion
  (5 shorter events, 0.1 us)
Async XLA Ops:
  7.2 2.1 %copy-start = (bf16[128,3584]{1,0:T(8,128)(2,1)S(1)}, bf16[128,3584]{1,0:T(8,128)(2,1)}, u32[]{:S(2)}) copy-start(bf16[128,3584]{1,0:T(8,128)(2,1)} %param.6) | copy-start | bytes 2752516
  7.2 116.5 %all-gather.2.cloned.1.call-start = ((), (), s32[]{:S(2)}) async-start(), calls=%async_computation.2 | async-start | bytes 8257536 | tf_op jit(solution)/shard_map/all_gather | solution.py:51
  8.7 0.6 copy-start.5
  77.0 1.3 copy-start.4
  77.0 1.5 copy-start.1
  78.3 1.5 copy-start.2
  81.0 77.9 %copy-start.3 = (bf16[1,128,3584]{1,2,0:T(8,128)(2,1)S(1)}, bf16[1,128,3584]{1,2,0:T(8,128)(2,1)}, u32[]{:S(2)}) copy-start(bf16[1,128,3584]{1,2,0:T(8,128)(2,1)} %copy.32) | copy-start | bytes 2752516
  143.2 29.1 %all-to-all-start.1 = ((f32[64,1,2]{2,1,0:T(1,128)}), f32[64,1,2]{2,1,0:T(1,128)S(1)}, u32[]{:S(2)}, u32[]{:S(2)}) async-start(f32[64,1,2]{2,1,0:T(1,128)} %bitcast.3), calls=%async_computation.1 | async-start | bytes 65536 | tf_op jit(solution)/shard_map/all_to_all | solution.py:72
  167.0 6.8 %copy-start.6 = (bf16[128]{0:T(256)(128)(2,1)S(1)}, bf16[128]{0:T(256)(128)(2,1)}, u32[]{:S(2)}) copy-start(bf16[128]{0:T(256)(128)(2,1)} %copy-done.5) | copy-start | bytes 772
Sparse Core Ops, SparseCore 0:
  78.4 45.2 all-gather.1
where the time goes:
time: 182 us; the launch traced here: 181 us
  blocking collectives  80.1 us (44%)
  waiting for transfers between devices  44.5 us (24%)
  starting transfers between devices  15.8 us (9%)
  between operations  14.2 us (8%)
  matrix products  13.1 us (7%)
  local copies, waits for them, and re-layouts  10.3 us (6%)
  other arithmetic  3.23 us (2%)
    all_to_all x1, blocking collectives, on_device(): lax.all_to_all(scaled_out.reshape(node_count, CAP, feature_count), 'node'...  66.9 us
    all_gather x1, waiting for transfers between devices, on_device(): lax.all_gather(arrived.reshape(node_count * CAP, feature_count), 'local',...  42.7 us
    all_to_all x1, starting transfers between devices, on_device(): lax.all_to_all(own_terms.reshape(node_count, CAP), 'node', split_axis=0,...  15.8 us
    psum x1, blocking collectives, on_device(): summed = lax.psum(score_terms, 'local')  13.2 us
    unnamed x20, local copies, waits for them, and re-layouts  7.28 us
    dot_general x1, matrix products, on_device(): lax.dot_general(hidden_now, scaled, (((0,), (0,)), ((), ())), preferred_e...  7.21 us
    dot_general x1, matrix products, on_device(): lax.dot_general(scaled, weight_now, (((1,), (1,)), ((), ())), preferred_e...  5.51 us
  transfers between devices with their start and end apart: 2, of which 2 were waited for; matrix products, arithmetic and copies ran while one was open for 8% of the time, Pallas kernels for 0%

commit v1 on v0

--- a/solution.py
+++ b/solution.py
@@ -10,6 +10,18 @@
 decay_rate = 0.1
 epsilon = 1e-08
 correct_second = 0.994079470779666
+
+
+def play_the_views(mine, comm_axis, dim_i):
+    return jnp.concatenate(
+        lax.all_to_all(
+            jnp.stack([mine] * lax.axis_size(comm_axis)),
+            axis_name=comm_axis,
+            split_axis=0,
+            concat_axis=0,
+        ),
+        axis=dim_i,
+    )
 
 
 def route(picked_experts, gate_values, node_count):
@@ -48,9 +60,7 @@
         concat_axis=0,
         tiled=True,
     )
-    scaled = lax.all_gather(
-        arrived.reshape(node_count * CAP, feature_count), "local", axis=0, tiled=True
-    )
+    scaled = play_the_views(arrived.reshape(node_count * CAP, feature_count), "local", 0)
     weight_now = down_weight[0]
     hidden_now = saved_hidden[0]
     hidden_f = lax.dot_general(

time: 182 us -> 205 us (1.13)
  the two profiles are of different devices: /device:TPU:8 before, /device:TPU:1 now
where the time goes in v1:
time: 205 us; the launch traced here: 204 us
  waiting for transfers between devices  81.6 us (40%)
  blocking collectives  77.2 us (38%)
  starting transfers between devices  15.1 us (7%)
  local copies, waits for them, and re-layouts  13.3 us (6%)
  matrix products  13.2 us (6%)
  other arithmetic  3.24 us (2%)
    all_to_all x1, waiting for transfers between devices, play_the_views(): lax.all_to_all(jnp.stack([mine] * lax.axis_size(comm_axis)), axis_name=co...  79.9 us
    all_to_all x1, blocking collectives, on_device(): lax.all_to_all(scaled_out.reshape(node_count, CAP, feature_count), 'node'...  64.6 us
    psum x1, blocking collectives, on_device(): summed = lax.psum(score_terms, 'local')  12.6 us
    all_to_all x1, starting transfers between devices, play_the_views(): lax.all_to_all(jnp.stack([mine] * lax.axis_size(comm_axis)), axis_name=co...  8.81 us
    unnamed x20, local copies, waits for them, and re-layouts  7.59 us
    dot_general x1, matrix products, on_device(): lax.dot_general(hidden_now, scaled, (((0,), (0,)), ((), ())), preferred_e...  7.23 us
    all_to_all x1, starting transfers between devices, on_device(): lax.all_to_all(own_terms.reshape(node_count, CAP), 'node', split_axis=0,...  6.28 us
    dot_general x1, matrix products, on_device(): lax.dot_general(scaled, weight_now, (((1,), (1,)), ((), ())), preferred_e...  5.6 us
  transfers between devices with their start and end apart: 2, of which 2 were waited for; matrix products, arithmetic and copies ran while one was open for 7% of the time, Pallas kernels for 0%

profile of v1, /device:TPU:1, one launch (start us, length us, event | category | flops | bytes accessed | tf_op | source)
XLA Modules:
  0.0 204.5 jit_solution(8396040006974670567)
XLA Ops:
  0.6 0.0 copy-start
  0.6 0.8 fusion.18
  1.5 0.2 convert_reduce_fusion
  1.6 0.7 select_reduce_fusion.2
  2.4 0.0 copy-start.5
  2.4 0.6 copy-done.5
  2.9 0.1 select_reduce_fusion.1
  3.0 0.0 copy-done
  3.1 0.4 fusion
  3.5 0.3 reshape.53
  3.8 64.6 %all_to_all.19 = bf16[64,2,3584]{2,1,0:T(2,128)(2,1)S(1)} all-to-all(bf16[64,2,3584]{2,1,0:T(2,128)(2,1)S(1)} %reshape.53), channel_id=1, replica_groups=mesh['node'=64,'local'=8] {'node'}, dimensions={0} | all-to-all | bytes 1835008 | tf_op jit(solution)/shard_map/all_to_all | solution.py:56
  68.4 0.3 stack_reshape.2
  68.7 3.6 %stack.3 = bf16[8,128,3584]{2,1,0:T(8,128)(2,1)} broadcast(bf16[128,3584]{1,0:T(8,128)(2,1)S(1)} %stack_reshape.2), dimensions={1,2} | broadcast | bytes 8257536 | tf_op jit(solution)/shard_map/stack | solution.py:18
  72.4 0.0 copy-start.4
  72.4 0.0 copy-start.2
  72.4 8.8 %all-to-all-start.1 = ((bf16[8,128,3584]{2,1,0:T(8,128)(2,1)}), bf16[8,128,3584]{2,1,0:T(8,128)(2,1)}, u32[]{:S(2)}, u32[]{:S(2)}) async-start(bf16[8,128,3584]{2,1,0:T(8,128)(2,1)} %stack.3), calls=%async_computation.1 | async-start | bytes 14680064 | tf_op jit(solution)/shard_map/all_to_all | solution.py:17
  81.2 0.0 copy-start.1
  81.2 0.0 copy-done.4
  81.2 0.1 copy.30
  81.3 0.0 copy-done.2
  81.3 1.3 copy.29
  82.6 0.0 copy-done.1
  82.6 1.3 copy.32
  83.9 79.9 %all-to-all-done.1 = bf16[8,128,3584]{2,1,0:T(8,128)(2,1)} async-done(((bf16[8,128,3584]{2,1,0:T(8,128)(2,1)}), bf16[8,128,3584]{2,1,0:T(8,128)(2,1)}, u32[]{:S(2)}, u32[]{:S(2)}) %all-to-all-start.1) | async-done | bytes 7340064 | tf_op jit(solution)/shard_map/all_to_all | solution.py:17
  163.8 0.0 copy-start.3
  163.8 5.6 %convert_bitcast_fusion = (bf16[1,1024,128]{1,2,0:T(8,128)(2,1)S(1)}, f32[1024]{0:T(1024)S(1)}) fusion(bf16[1,1024,128]{1,2,0:T(8,128)(2,1)S(1)} %copy.30, bf16[1024,3584]{1,0:T(8,128)(2,1)} %bitcast, bf16[1,128,3584]{2,1,0:T(8,128)(2,1)S(1)} %copy-done.2), kind=kOutput, calls=%fused_computation.17 | convolution fusion | flops 940047360 | bytes 8785920 | tf_op jit(solution)/shard_map/dot_general | solution.py:66
  169.4 12.6 %psum.7 = f32[8,128]{1,0:T(8,128)S(1)} all-reduce(f32[8,128]{1,0:T(8,128)S(1)} %bitcast.42), channel_id=1, replica_groups=mesh['node'=64,'local'=8] {'local'}, use_global_device_ids=true, to_apply=%region_6.7 | all-reduce | flops 1024 | bytes 8192 | tf_op jit(solution)/shard_map/psum | solution.py:80
  182.1 0.7 all_to_all.14
  182.8 6.3 %all-to-all-start.2 = ((f32[64,1,2]{2,1,0:T(1,128)}), f32[64,1,2]{2,1,0:T(1,128)S(1)}, u32[]{:S(2)}, u32[]{:S(2)}) async-start(f32[64,1,2]{2,1,0:T(1,128)} %bitcast.4), calls=%async_computation.2 | async-start | bytes 65536 | tf_op jit(solution)/shard_map/all_to_all | solution.py:82
  189.1 0.0 copy-done.3
  189.1 7.2 %fusion.6 = (bf16[1,128,3584]{1,2,0:T(8,128)(2,1)S(1)}, bf16[1,128,3584]{1,2,0:T(8,128)(2,1)}) fusion(bf16[1,128,3584]{1,2,0:T(8,128)(2,1)} %copy.32, bf16[1,128,3584]{1,2,0:T(8,128)(2,1)S(1)} %copy-done.3, bf16[1024,3584]{1,0:T(8,128)(2,1)} %bitcast, bf16[1,1024,128]{2,1,0:T(8,128)(2,1)S(1)} %copy-done.4), kind=kOutput, calls=%fused_computation.11 | convolution fusion | flops 946405376 | bytes 11272192 | tf_op jit(solution)/shard_map/dot_general | solution.py:70
  196.3 0.0 copy-start.6
  196.3 2.2 %copy.34 = bf16[1,128,3584]{2,1,0:T(8,128)(2,1)} copy(bf16[1,128,3584]{1,2,0:T(8,128)(2,1)} %get-tuple-element.23) | data formatting | bytes 1835008
  198.6 1.3 copy.35
  199.8 0.8 copy.33
  200.7 1.7 all-to-all-done.2
  202.4 0.5 broadcast.40
  202.9 0.7 reduce.7
  203.6 0.1 broadcast_in_dim.70
  203.7 0.1 select_reduce_fusion
  203.8 0.0 copy-done.6
  203.9 0.6 broadcast_select_fusion
  (5 shorter events, 0.1 us)
Async XLA Ops:
  0.6 2.4 %copy-start = (bf16[128,3584]{1,0:T(8,128)(2,1)S(1)}, bf16[128,3584]{1,0:T(8,128)(2,1)}, u32[]{:S(2)}) copy-start(bf16[128,3584]{1,0:T(8,128)(2,1)} %param.6) | copy-start | bytes 2752516
  2.4 0.6 copy-start.5
  72.4 8.8 %copy-start.4 = (bf16[1,1024,128]{2,1,0:T(8,128)(2,1)S(1)}, bf16[1,1024,128]{2,1,0:T(8,128)(2,1)}, u32[]{:S(2)}) copy-start(bf16[1,1024,128]{2,1,0:T(8,128)(2,1)} %param.9) | copy-start | bytes 786436
  72.4 9.0 %copy-start.2 = (bf16[1,128,3584]{2,1,0:T(8,128)(2,1)S(1)}, bf16[1,128,3584]{2,1,0:T(8,128)(2,1)}, u32[]{:S(2)}) copy-start(bf16[1,128,3584]{2,1,0:T(8,128)(2,1)} %param.10) | copy-start | bytes 2752516
  72.4 91.4 %all-to-all-start.1 = ((bf16[8,128,3584]{2,1,0:T(8,128)(2,1)}), bf16[8,128,3584]{2,1,0:T(8,128)(2,1)}, u32[]{:S(2)}, u32[]{:S(2)}) async-start(bf16[8,128,3584]{2,1,0:T(8,128)(2,1)} %stack.3), calls=%async_computation.1 | async-start | bytes 14680064 | tf_op jit(solution)/shard_map/all_to_all | solution.py:17
  81.2 1.4 copy-start.1
  163.8 25.3 %copy-start.3 = (bf16[1,128,3584]{1,2,0:T(8,128)(2,1)S(1)}, bf16[1,128,3584]{1,2,0:T(8,128)(2,1)}, u32[]{:S(2)}) copy-start(bf16[1,128,3584]{1,2,0:T(8,128)(2,1)} %copy.29) | copy-start | bytes 2752516
  182.8 19.5 %all-to-all-start.2 = ((f32[64,1,2]{2,1,0:T(1,128)}), f32[64,1,2]{2,1,0:T(1,128)S(1)}, u32[]{:S(2)}, u32[]{:S(2)}) async-start(f32[64,1,2]{2,1,0:T(1,128)} %bitcast.4), calls=%async_computation.2 | async-start | bytes 65536 | tf_op jit(solution)/shard_map/all_to_all | solution.py:82
  196.3 7.5 %copy-start.6 = (bf16[128]{0:T(256)(128)(2,1)S(1)}, bf16[128]{0:T(256)(128)(2,1)}, u32[]{:S(2)}) copy-start(bf16[128]{0:T(256)(128)(2,1)} %copy-done.5) | copy-start | bytes 772
